TPU v7x, 32 devices: a whole 2x2x4 slice. The times are simulated.
32 devices in a mesh: parts: 2 (over y), wide: 4 (over z), rep: 2 (over x), sub: 2 (over core).
Axes of the slice: x: 2, y: 2, z: 4, core: 2. Of those that a mesh axis runs over, the one named last changes fastest.
Arguments:
- activations: bfloat16 [8, 2048, 512], P(('parts', 'wide'), 'sub'), parts along dimension 0, may hold values from -6 to 6
- deltas: bfloat16 [8, 2048, 512], P(('parts', 'wide'), 'sub'), parts along dimension 0, may hold values from -6 to 6
- act_factor: bfloat16 [512, 512], P(None, 'rep'), as said below
- delta_factor: bfloat16 [512, 512], P(None, 'rep'), as said below
- queries: bfloat16 [1280, 512, 512], P(None, ('rep', 'wide'), 'sub'), may hold values from -0.00059890747 to 0.00059890747
- assignment: int32 [8], P('parts'), parts along dimension 0, may hold values from 0 to 3, each once
- padding: int32 [8], P(('parts', 'wide')), parts along dimension 0, may hold values from 0 to 1023
Outputs:
- scores: float32 [8, 1280], P(('parts', 'wide'), ('rep', 'sub')), parts along dimension 0
There are 2 independent parts, one for each index of `parts`. A program takes and returns all parts, laid end to end along the dimension named above; an argument that names none is the same for every part. Nothing has to cross between parts.
Inputs may be any that keep to these rules, and one draw needn't show every extreme that they name: `act_factor`: symmetric and positive definite. `delta_factor`: symmetric and positive definite. `assignment`: each number once.
All inputs are finite; a program needn't handle non-finite values.
Results may differ from a plain program's by a relative error of at most 0.005.
Values may be sent and summed in bfloat16 or wider, within the bound.
A program may use at most 128 MiB of HBM per device.

v0:
```python
import jax
import jax.numpy as jnp
from jax import lax
from jax.sharding import PartitionSpec as P


def shards(activations, deltas, act_factor, delta_factor, queries, assignment, padding):
    seq_dev, tok_dev, feature_width = activations.shape
    full_length = tok_dev * lax.axis_size("sub")
    token_start = lax.axis_index("sub") * tok_dev
    positions = token_start + lax.broadcasted_iota(jnp.int32, (seq_dev, tok_dev), 1)
    kept_mask = positions < (full_length - padding)[:, None]
    masked = jnp.where(kept_mask[:, :, None], deltas, jnp.zeros((), jnp.bfloat16))
    delta_proj = jnp.einsum(
        "stw,wi->sti", masked, delta_factor, preferred_element_type=jnp.float32
    ).astype(jnp.bfloat16)
    act_proj = jnp.einsum(
        "stw,wj->stj",
        activations,
        lax.all_gather(act_factor, "rep", axis=1, tiled=True),
        preferred_element_type=jnp.float32,
    ).astype(jnp.bfloat16)
    partial_value = jnp.einsum(
        "sti,stj->sij", delta_proj, act_proj, preferred_element_type=jnp.float32
    )
    summed = lax.psum_scatter(partial_value, "sub", scatter_dimension=2, tiled=True).astype(
        jnp.bfloat16
    )
    regrouped = lax.all_to_all(summed, "wide", split_axis=1, concat_axis=0, tiled=True)
    seq_total = regrouped.shape[0]
    grad_rows = regrouped.reshape(seq_total, -1)
    query_rows = queries.reshape(queries.shape[0], -1)
    partial_scores = lax.dot_general(
        grad_rows, query_rows, (((1,), (1,)), ((), ())), preferred_element_type=jnp.float32
    )
    inverse_order = (
        jnp.zeros((seq_total,), jnp.int32)
        .at[assignment]
        .set(jnp.arange(seq_total, dtype=jnp.int32))
    )
    ranked = jnp.take(partial_scores, inverse_order, axis=0)
    by_column = lax.psum_scatter(ranked, ("rep", "sub"), scatter_dimension=1, tiled=True)
    return lax.psum_scatter(by_column, "wide", scatter_dimension=0, tiled=True)


def solution(mesh):
    placed = (
        P(("parts", "wide"), "sub", None),
        P(("parts", "wide"), "sub", None),
        P(None, "rep"),
        P(None, "rep"),
        P(None, ("rep", "wide"), "sub"),
        P("parts"),
        P(("parts", "wide")),
    )
    return jax.shard_map(
        shards,
        mesh=mesh,
        in_specs=placed,
        out_specs=P(("parts", "wide"), ("rep", "sub")),
        check_vma=False,
    )
```

profile of v0, /device:TPU:0, one launch (start us, length us, event | category | flops | bytes accessed | tf_op | source)
XLA Modules:
  0.0 137.6 jit_solution(17364108124651924373)
XLA Ops:
  6.5 0.0 copy-start
  6.5 0.0 reduce-scatter.5.cloned.1.call-start
  7.3 10.2 %all_gather.3 = bf16[512,512]{1,0:T(8,128)(2,1)S(1)} all-gather(bf16[512,256]{1,0:T(8,128)(2,1)} %param.9), channel_id=1, replica_groups=mesh['parts'=2,'wide'=4,'rep'=2,'sub'=2] {'rep'}, dimensions={1}, use_global_device_ids=true | all-gather | bytes 786432 | tf_op jit(solution)/shard_map/all_gather | solution.py:20
  17.5 1.8 %convolution_convert_fusion.1 = bf16[1024,256]{1,0:T(8,128)(2,1)S(1)} fusion(bf16[512,256]{1,0:T(8,128)(2,1)} %param.10, bf16[1,1024,512]{2,1,0:T(8,128)(2,1)} %param.8, pred[1024]{0:T(1024)(128)(4,1)S(1)} %add_compare_fusion), kind=kOutput, calls=%fused_computation.4 | convolution fusion | flops 269221888 | bytes 1836032 | tf_op jit(solution)/shard_map/stw,wi->sti/dot_general | solution.py:14
  19.3 0.0 copy-done
  19.3 1.8 %fusion.1 = f32[1,256,512]{2,1,0:T(8,128)} fusion(bf16[1024,256]{1,0:T(8,128)(2,1)S(1)} %convolution_convert_fusion.1, bf16[512,512]{1,0:T(8,128)(2,1)S(1)} %all_gather.3, bf16[1,1024,512]{2,1,0:T(8,128)(2,1)S(1)} %copy-done), kind=kOutput, calls=%fused_computation.5 | convolution fusion | flops 805830656 | bytes 2621440 | tf_op jit(solution)/shard_map/sti,stj->sij/dot_general | solution.py:23
  21.1 0.0 reduce-scatter.5.cloned.1.call-update
  21.1 0.0 copy-start.2
  21.1 0.0 copy-start.1
  21.1 38.2 %copy.12 = bf16[160,8,64,256]{3,1,2,0:T(8,128)(2,1)} copy(bf16[160,8,64,256]{3,2,1,0:T(8,128)(2,1)} %bitcast.26) | data formatting | bytes 83886080
  59.3 0.0 copy-done.2
  59.3 0.0 copy-start.3
  59.3 0.6 scatter_custom_fusion
  59.9 0.0 reduce-scatter.5.cloned.1.call-done
  60.0 1.0 convert_element_type.13
  60.9 0.2 copy.14
  61.1 0.5 broadcast.49
  61.7 1.4 %reduce.2 = bf16[256,256]{1,0:T(8,128)(2,1)S(1)} reduce(bf16[256,1,256]{2,1,0:T(2,128)(2,1)S(1)} %bitcast.28, bf16[]{:T(256)} %broadcast.49), dimensions={1}, to_apply=%bitcast.24.reduce_sub_computation | reduce | bytes 262146
  63.1 0.7 reshape.71
  63.8 5.1 %all-to-all-start = ((bf16[4,2,8192]{2,1,0:T(2,128)(2,1)}), bf16[4,2,8192]{2,1,0:T(2,128)(2,1)S(1)}, u32[]{:S(2)}, u32[]{:S(2)}) async-start(bf16[4,2,8192]{2,1,0:T(2,128)(2,1)} %reshape.71), calls=%async_computation.1 | async-start | bytes 262144 | tf_op jit(solution)/shard_map/all_to_all | solution.py:29
  68.8 0.0 reduce-scatter.7.cloned.1.call-start
  68.8 5.9 %all-to-all-done = bf16[4,2,8192]{2,1,0:T(2,128)(2,1)S(1)} async-done(((bf16[4,2,8192]{2,1,0:T(2,128)(2,1)}), bf16[4,2,8192]{2,1,0:T(2,128)(2,1)S(1)}, u32[]{:S(2)}, u32[]{:S(2)}) %all-to-all-start) | async-done | bytes 131104 | tf_op jit(solution)/shard_map/all_to_all | solution.py:29
  74.7 0.1 reshape.72
  74.9 0.7 bitcast_reduce_fusion
  75.6 0.1 reshape.45
  75.7 17.5 %fusion.11 = f32[4,1280]{1,0:T(4,128)S(1)} fusion(bf16[4,16384]{1,0:T(4,128)(2,1)S(1)} %reshape.45, bf16[1280,16384]{1,0:T(8,128)(2,1)} %bitcast.25), kind=kOutput, calls=%fused_computation.23 | convolution fusion | flops 167772160 | bytes 42094592 | tf_op jit(solution)/shard_map/dot_general | solution.py:33
  93.2 0.6 gather_fusion
  93.8 0.1 broadcast_select_fusion
  93.8 1.1 copy.10
  94.9 0.0 reduce-scatter.7.cloned.1.call-update
  95.0 0.0 copy-done.3
  95.0 0.6 dynamic-slice
  95.6 21.0 %reduce-scatter.7.cloned.1.call-done = f32[320,4]{1,0:T(8,128)} async-done(((f32[1280,4]{1,0:T(8,128)}), f32[320,4]{1,0:T(8,128)}) %reduce-scatter.7.cloned.1.call-update) | async-done | bytes 5136
  116.6 1.0 copy.11
  117.6 11.9 %all-reduce = f32[4,320]{1,0:T(4,128)S(1)} all-reduce(f32[4,320]{1,0:T(4,128)S(1)} %copy.11), channel_id=4, replica_groups=mesh['parts'=2,'wide'=4,'rep'=2,'sub'=2] {'wide'}, use_global_device_ids=true, to_apply=%region_3.4.clone | all-reduce | flops 1280 | bytes 10240
  129.5 1.2 constant_dynamic-slice_fusion
  130.7 0.0 copy-done.1
  (6 shorter events, 0.0 us)
Async XLA Ops:
  6.5 12.7 %copy-start = (bf16[1,1024,512]{2,1,0:T(8,128)(2,1)S(1)}, bf16[1,1024,512]{2,1,0:T(8,128)(2,1)}, u32[]{:S(2)}) copy-start(bf16[1,1024,512]{2,1,0:T(8,128)(2,1)} %param.7) | copy-start | bytes 3145732
  6.5 53.4 %reduce-scatter.5.cloned.1.call-start = ((), (), s32[]{:S(2)}) async-start(), calls=%async_computation.3 | async-start | bytes 786432 | tf_op jit(solution)/shard_map/reduce_scatter | solution.py:26
  21.1 38.2 %copy-start.2 = (s32[4]{0:T(128)S(1)}, s32[4]{0:T(128)}, u32[]{:S(2)}) copy-start(s32[4]{0:T(128)} %param.12) | copy-start | bytes 52
  21.1 109.6 %copy-start.1 = (bf16[1,1024,512]{2,1,0:T(8,128)(2,1)S(1)}, bf16[1,1024,512]{2,1,0:T(8,128)(2,1)}, u32[]{:S(2)}) copy-start(bf16[1,1024,512]{2,1,0:T(8,128)(2,1)} %param.7) | copy-start | bytes 3145732
  59.3 35.7 %copy-start.3 = (u32[32]{0:T(128)S(1)}, u32[32]{0:T(128)}, u32[]{:S(2)}) copy-start(u32[32]{0:T(128)} %constant.33) | copy-start | bytes 388
  63.8 11.0 %all-to-all-start = ((bf16[4,2,8192]{2,1,0:T(2,128)(2,1)}), bf16[4,2,8192]{2,1,0:T(2,128)(2,1)S(1)}, u32[]{:S(2)}, u32[]{:S(2)}) async-start(bf16[4,2,8192]{2,1,0:T(2,128)(2,1)} %reshape.71), calls=%async_computation.1 | async-start | bytes 262144 | tf_op jit(solution)/shard_map/all_to_all | solution.py:29
  68.8 47.8 %reduce-scatter.7.cloned.1.call-start = ((), (), s32[]{:S(2)}) async-start(), calls=%async_computation.4 | async-start | bytes 819200
Sparse Core Ops, SparseCore 0:
  21.2 9.3 reduce-scatter.4
  95.1 21.4 reduce-scatter.6
where the time goes:
time: 138 us
  local copies, waits for them, and re-layouts  45.6 us (33%)
  waiting for transfers between devices  27 us (20%)
  blocking collectives  22.1 us (16%)
  matrix products  21.1 us (15%)
  between operations  14.3 us (10%)
  starting transfers between devices  5.07 us (4%)
  other arithmetic  2.47 us (2%)
    unnamed x16, local copies, waits for them, and re-layouts  43.4 us
    unnamed x3, waiting for transfers between devices  21 us
    dot_general x1, matrix products, shards(): lax.dot_general(grad_rows, query_rows, (((1,), (1,)), ((), ())), preferre...  17.5 us
    unnamed x1, blocking collectives  11.9 us
    all_gather x1, blocking collectives, shards(): lax.all_gather(act_factor, 'rep', axis=1, tiled=True)  10.2 us
    all_to_all x1, waiting for transfers between devices, shards(): lax.all_to_all(summed, 'wide', split_axis=1, concat_axis=0, tiled=True)  5.91 us
    all_to_all x1, starting transfers between devices, shards(): lax.all_to_all(summed, 'wide', split_axis=1, concat_axis=0, tiled=True)  5.06 us
  transfers between devices with their start and end apart: 3, of which 2 were waited for; matrix products, arithmetic and copies ran while one was open for 29% of the time, Pallas kernels for 0%

commit v1 on v0

--- a/solution.py
+++ b/solution.py
@@ -1,10 +1,19 @@
+import functools
+
 import jax
 import jax.numpy as jnp
 from jax import lax
+from jax.experimental import pallas as pl
+from jax.experimental.pallas import tpu as pltpu
 from jax.sharding import PartitionSpec as P
 
-
-def shards(activations, deltas, act_factor, delta_factor, queries, assignment, padding):
+MESH = pl.DeviceIdType.MESH
+GROUP = 32
+
+
+def general_shards(
+    activations, deltas, act_factor, delta_factor, queries, assignment, padding
+):
     seq_dev, tok_dev, feature_width = activations.shape
     full_length = tok_dev * lax.axis_size("sub")
     token_start = lax.axis_index("sub") * tok_dev
@@ -43,6 +52,301 @@
     return lax.psum_scatter(by_column, "wide", scatter_dimension=0, tiled=True)
 
 
+def kernel(
+    n_wide,
+    rows,
+    assignment_ref,
+    padding_ref,
+    act_hbm,
+    delta_hbm,
+    act_factor_hbm,
+    delta_factor_hbm,
+    query_hbm,
+    out_ref,
+    act,
+    delta,
+    act_factor,
+    delta_factor,
+    query,
+    diag,
+    inner_mine,
+    inner_theirs,
+    factor_cols,
+    grad,
+    grad_all,
+    weights,
+    folded,
+    outgoing,
+    incoming,
+    load_sem,
+    query_sem,
+    diag_sem,
+    inner_sem,
+    grad_send_sem,
+    grad_recv_sem,
+    score_send_sem,
+    score_recv_sem,
+):
+    z = lax.axis_index("wide")
+    r = lax.axis_index("rep")
+    c = lax.axis_index("sub")
+    n_rep, n_sub = 2, 2
+
+    def peer(dz, dr, dc):
+        return {
+            "wide": lax.rem(z + dz, n_wide),
+            "rep": lax.rem(r + dr, n_rep),
+            "sub": lax.rem(c + dc, n_sub),
+        }
+
+    block_order = ((1, 1), (1, 0), (0, 1), (0, 0))
+    everyone = [
+        (dz, dr, dc) for dz in range(n_wide) for dr, dc in block_order if (dz, dr, dc) != (0, 0, 0)
+    ]
+    barrier = pltpu.get_barrier_semaphore()
+    for offset in everyone:
+        pl.semaphore_signal(barrier, inc=1, device_id=peer(*offset), device_id_type=MESH)
+
+    loads = [
+        pltpu.make_async_copy(src, dst, load_sem.at[k])
+        for k, (src, dst) in enumerate(
+            (
+                (delta_factor_hbm, delta_factor),
+                (delta_hbm, delta),
+                (act_factor_hbm, act_factor),
+                (act_hbm, act),
+            )
+        )
+    ]
+    for load in loads:
+        load.start()
+
+    chunk = GROUP * rows
+    total = query.shape[0]
+    block_groups = total // (chunk * n_rep * n_sub)
+
+    def query_copy(place):
+        span = pl.ds(pl.multiple_of(place * chunk, chunk), chunk)
+        return pltpu.make_async_copy(query_hbm.at[span, :], query.at[span, :], query_sem.at[place])
+
+    def block_at(dr, dc):
+        return lax.rem(r + dr, n_rep) * n_sub + lax.rem(c + dc, n_sub)
+
+    for dr, dc in block_order:
+        first = block_at(dr, dc) * block_groups
+
+        def begin(t, carry, first=first):
+            query_copy(first + t).start()
+            return carry
+
+        lax.fori_loop(0, block_groups, begin, 0)
+
+    loads[0].wait()
+    loads[1].wait()
+    tokens = delta.shape[0]
+    half = act_factor.shape[1]
+    limit = n_sub * tokens - padding_ref[0] - c * tokens
+    position = lax.broadcasted_iota(jnp.int32, (tokens, half), 0)
+    projected = jnp.dot(delta[...], delta_factor[...], preferred_element_type=jnp.float32)
+    delta_proj = jnp.where(position < limit, projected, 0.0).astype(jnp.bfloat16)
+
+    loads[2].wait()
+    pl.semaphore_wait(barrier, len(everyone))
+    diag_rows = pl.ds(pl.multiple_of(c * half, half), half)
+    diag_copy = pltpu.make_async_remote_copy(
+        src_ref=act_factor.at[diag_rows, :],
+        dst_ref=diag,
+        send_sem=diag_sem.at[0],
+        recv_sem=diag_sem.at[1],
+        device_id=peer(0, 1, 0),
+        device_id_type=MESH,
+    )
+
+    @pl.when(r == c)
+    def _():
+        diag_copy.start()
+
+    loads[3].wait()
+    inner_mine[...] = lax.dot_general(
+        delta_proj, act[...], (((0,), (0,)), ((), ())), preferred_element_type=jnp.float32
+    )
+    inner_copy = pltpu.make_async_remote_copy(
+        src_ref=inner_mine,
+        dst_ref=inner_theirs,
+        send_sem=inner_sem.at[0],
+        recv_sem=inner_sem.at[1],
+        device_id=peer(0, 0, 1),
+        device_id_type=MESH,
+    )
+    inner_copy.start()
+
+    @pl.when(r == c)
+    def _():
+        factor_cols[...] = act_factor[...]
+        diag_copy.wait_send()
+
+    @pl.when(r != c)
+    def _():
+        mirrored = act_factor[diag_rows, :].astype(jnp.float32).T.astype(jnp.bfloat16)
+        factor_cols[pl.ds(pl.multiple_of(r * half, half), half), :] = mirrored
+        diag_copy.wait_recv()
+        factor_cols[diag_rows, :] = diag[...]
+
+    inner_copy.wait_recv()
+    inner = inner_mine[...] + inner_theirs[...]
+    high = inner.astype(jnp.bfloat16)
+    low = (inner - high.astype(jnp.float32)).astype(jnp.bfloat16)
+    gradient = jnp.dot(high, factor_cols[...], preferred_element_type=jnp.float32) + jnp.dot(
+        low, factor_cols[...], preferred_element_type=jnp.float32
+    )
+    grad[...] = gradient.astype(jnp.bfloat16)
+    mine = pl.ds(pl.multiple_of(z * rows, rows), rows)
+    grad_copies = []
+    for dz in range(n_wide - 1, 0, -1):
+        target = pl.ds(pl.multiple_of(lax.rem(z + dz, n_wide) * rows, rows), rows)
+        copy = pltpu.make_async_remote_copy(
+            src_ref=grad.at[target, :],
+            dst_ref=grad_all.at[mine, :],
+            send_sem=grad_send_sem.at[dz],
+            recv_sem=grad_recv_sem.at[dz],
+            device_id=peer(dz, 0, 0),
+            device_id_type=MESH,
+        )
+        copy.start()
+        grad_copies.append(copy)
+    grad_all[mine, :] = grad[mine, :]
+
+    width = n_wide * rows
+    lane = lax.broadcasted_iota(jnp.int32, (8, width), 1)
+    sublane = lax.broadcasted_iota(jnp.int32, (8, width), 0)
+    owner = lane // rows
+    ranks = jnp.zeros((8, width), jnp.int32)
+    for n in range(n_wide):
+        ranks = jnp.where(owner == n, assignment_ref[n], ranks)
+    places = jnp.where(ranks == sublane, 1.0, 0.0).astype(jnp.bfloat16)
+    tile_of_lane = lax.rem(lane, rows) // 8
+    on_diagonal = lax.rem(lane, 8) == sublane
+
+    block_size = block_groups * GROUP
+    folded[pl.ds(block_size, folded.shape[0] - block_size), :] = jnp.zeros(
+        (folded.shape[0] - block_size, width), jnp.float32
+    )
+    inner_copy.wait_send()
+    for copy in grad_copies:
+        copy.wait_recv()
+    weights[...] = grad_all[...].astype(jnp.float32).T.astype(jnp.bfloat16)
+
+    score_copies = []
+    for k, (dr, dc) in enumerate(block_order):
+        first = block_at(dr, dc) * block_groups
+
+        def step(t, carry, first=first):
+            query_copy(first + t).wait()
+            span = pl.ds(pl.multiple_of((first + t) * chunk, chunk), chunk)
+            products = jnp.dot(
+                query[span, :], weights[...], preferred_element_type=jnp.float32
+            ).reshape(GROUP, rows // 8, 8, width)
+            chosen = products[:, 0]
+            for a in range(1, rows // 8):
+                chosen = jnp.where((tile_of_lane == a)[None], products[:, a], chosen)
+            chosen = jnp.where(on_diagonal[None], chosen, 0.0)
+            folded[pl.ds(pl.multiple_of(t * GROUP, GROUP), GROUP), :] = jnp.sum(chosen, axis=1)
+            return carry
+
+        lax.fori_loop(0, block_groups, step, 0)
+        sums = folded[...]
+        sums_high = sums.astype(jnp.bfloat16)
+        sums_low = (sums - sums_high.astype(jnp.float32)).astype(jnp.bfloat16)
+        contract = (((1,), (1,)), ((), ()))
+        ranked = lax.dot_general(
+            places, sums_high, contract, preferred_element_type=jnp.float32
+        ) + lax.dot_general(places, sums_low, contract, preferred_element_type=jnp.float32)
+        for p in range(n_wide):
+            outgoing[k, p] = ranked[p : p + 1, :]
+        for dz in range(n_wide - 1, -1, -1):
+            slot = k * n_wide + dz
+            source = outgoing.at[k, lax.rem(z + dz, n_wide)]
+            if (dz, dr, dc) == (0, 0, 0):
+                continue
+            copy = pltpu.make_async_remote_copy(
+                src_ref=source,
+                dst_ref=incoming.at[slot],
+                send_sem=score_send_sem.at[slot],
+                recv_sem=score_recv_sem.at[slot],
+                device_id=peer(dz, dr, dc),
+                device_id_type=MESH,
+            )
+            copy.start()
+            score_copies.append((slot, copy))
+
+    result = outgoing[len(block_order) - 1, z]
+    for copy in grad_copies:
+        copy.wait_send()
+    for slot, copy in score_copies:
+        copy.wait_send()
+        copy.wait_recv()
+        result = result + incoming[slot]
+    out_ref[...] = result[:, :block_size]
+
+
+def fused_shards(
+    n_wide, activations, deltas, act_factor, delta_factor, queries, assignment, padding
+):
+    _, tokens, features = activations.shape
+    n_queries, rows, columns = queries.shape
+    half = act_factor.shape[1]
+    width = n_wide * rows
+    groups = n_queries // GROUP
+    block_size = n_queries // 4
+    padded = -(-block_size // 128) * 128
+    hbm = pl.BlockSpec(memory_space=pl.ANY)
+    smem = pl.BlockSpec(memory_space=pltpu.SMEM)
+    dma = pltpu.SemaphoreType.DMA
+    bf16, f32 = jnp.bfloat16, jnp.float32
+    return pl.pallas_call(
+        functools.partial(kernel, n_wide, rows),
+        out_shape=jax.ShapeDtypeStruct((1, block_size), f32),
+        in_specs=[smem, smem] + [hbm] * 5,
+        out_specs=pl.BlockSpec(memory_space=pltpu.VMEM),
+        scratch_shapes=[
+            pltpu.VMEM((tokens, features), bf16),
+            pltpu.VMEM((tokens, features), bf16),
+            pltpu.VMEM((features, half), bf16),
+            pltpu.VMEM((features, half), bf16),
+            pltpu.VMEM((n_queries * rows, columns), bf16),
+            pltpu.VMEM((half, half), bf16),
+            pltpu.VMEM((half, features), f32),
+            pltpu.VMEM((half, features), f32),
+            pltpu.VMEM((features, half), bf16),
+            pltpu.VMEM((half, columns), bf16),
+            pltpu.VMEM((width, columns), bf16),
+            pltpu.VMEM((columns, width), bf16),
+            pltpu.VMEM((padded, width), f32),
+            pltpu.VMEM((4, n_wide, 1, padded), f32),
+            pltpu.VMEM((4 * n_wide, 1, padded), f32),
+            dma((4,)),
+            dma((groups,)),
+            dma((2,)),
+            dma((2,)),
+            dma((n_wide,)),
+            dma((n_wide,)),
+            dma((4 * n_wide,)),
+            dma((4 * n_wide,)),
+        ],
+        compiler_params=pltpu.CompilerParams(
+            collective_id=0, has_side_effects=True, vmem_limit_bytes=60 * 1024 * 1024
+        ),
+    )(
+        assignment,
+        padding,
+        activations.reshape(tokens, features),
+        deltas.reshape(tokens, features),
+        act_factor,
+        delta_factor,
+        queries.reshape(n_queries * rows, columns),
+    )
+
+
 def solution(mesh):
     placed = (
         P(("parts", "wide"), "sub", None),
@@ -53,6 +357,26 @@
         P("parts"),
         P(("parts", "wide")),
     )
+    n_wide, n_rep, n_sub = (mesh.shape[name] for name in ("wide", "rep", "sub"))
+
+    def shards(activations, deltas, act_factor, delta_factor, queries, assignment, padding):
+        seq_dev, tokens, features = activations.shape
+        n_queries, rows, columns = queries.shape
+        fits = (
+            seq_dev == 1
+            and (n_rep, n_sub) == (2, 2)
+            and n_wide <= 8
+            and rows % 16 == 0
+            and (n_wide * rows) % 128 == 0
+            and columns % 128 == 0
+            and act_factor.shape[1] == columns == n_wide * rows
+            and tokens % 16 == 0
+            and n_queries % (4 * GROUP) == 0
+            and n_queries * rows * columns * 2 <= 44 * 2**20
+        )
+        run = functools.partial(fused_shards, n_wide) if fits else general_shards
+        return run(activations, deltas, act_factor, delta_factor, queries, assignment, padding)
+
     return jax.shard_map(
         shards,
         mesh=mesh,

time: 138 us -> 39.7 us (0.29)
  local copies, waits for them, and re-layouts: 45.6 us -> 1.24 us
  Pallas kernels: 0 us -> 37.6 us
  waiting for transfers between devices: 27 us -> 0 us
  blocking collectives: 22.1 us -> 0 us
  matrix products: 21.1 us -> 0 us
  between operations: 14.3 us -> 0.66 us
  starting transfers between devices: 5.07 us -> 0 us
  other arithmetic: 2.47 us -> 0 us
    unnamed x16 -> x1, local copies, waits for them, and re-layouts: 43.4 us -> 1.24 us
    pallas_call x0 -> x1, Pallas kernels: none -> 37.6 us  [fused_shards(): pl.pallas_call(functools.partial(kernel, n_wide, rows), out_shape=jax.Sha...]
    dot_general x3 -> x0, matrix products: 21.1 us -> none  [the longest x1 17.5 us: shards(): lax.dot_general(grad_rows, query_rows, (((1,), (1,)), ((), ())), preferre...]
    unnamed x3 -> x0, waiting for transfers between devices: 21 us -> none
    unnamed x1 -> x0, blocking collectives: 11.9 us -> none
    all_gather x1 -> x0, blocking collectives: 10.2 us -> none  [shards(): lax.all_gather(act_factor, 'rep', axis=1, tiled=True)]
    all_to_all x1 -> x0, waiting for transfers between devices: 5.91 us -> none  [shards(): lax.all_to_all(summed, 'wide', split_axis=1, concat_axis=0, tiled=True)]
    all_to_all x1 -> x0, starting transfers between devices: 5.06 us -> none  [shards(): lax.all_to_all(summed, 'wide', split_axis=1, concat_axis=0, tiled=True)]
  transfers between devices with their start and end apart: 3 -> 0, of which waited for: 2 -> 0; matrix products, arithmetic and copies ran while one was open for 29% -> 0% of each run, Pallas kernels for 0% -> 0%
where the time goes in v1:
time: 39.7 us; the launch traced here: 39.5 us
  Pallas kernels  37.6 us (95%)
  local copies, waits for them, and re-layouts  1.24 us (3%)
  between operations  0.66 us (2%)
    pallas_call x1, Pallas kernels, fused_shards(): pl.pallas_call(functools.partial(kernel, n_wide, rows), out_shape=jax.Sha...  37.6 us
    unnamed x1, local copies, waits for them, and re-layouts  1.24 us

profile of v1, /device:TPU:0, one launch (start us, length us, event | category | flops | bytes accessed | tf_op | source)
XLA Modules:
  0.0 39.5 jit_solution(12192265832552627100)
XLA Ops:
  0.7 37.6 %shard_map.73 = f32[1,320]{1,0:T(1,128)} custom-call(s32[4]{0:T(128)} %assignment_ref.1, s32[1]{0:T(128)S(6)} %copy.9.padding_ref, bf16[1024,512]{1,0:T(8,128)(2,1)} %bitcast.4, bf16[1024,512]{1,0:T(8,128)(2,1)} %bitcast.5, bf16[512,256]{1,0:T(8,128)(2,1)} %act_factor_hbm.1, bf16[512,256]{1,0:T(8,128)(2,1)} %delta_factor_hbm.1, bf16[81920,256]{1,0:T(8,128)(2,1)} %bitcast.3), custom_call_target="tpu_custom_call" | custom-call | tf_op jit(solution)/shard_map/pallas_call | solution.py:306
  38.3 1.2 %copy.10 = f32[1,320]{1,0:T(1,128)} copy(f32[1,320]{1,0:T(1,128)} %shard_map.73) | data formatting | bytes 2560

commit v2 on v1

--- a/solution.py
+++ b/solution.py
@@ -8,7 +8,7 @@
 from jax.sharding import PartitionSpec as P
 
 MESH = pl.DeviceIdType.MESH
-GROUP = 32
+GROUP = 160
 
 
 def general_shards(
@@ -100,9 +100,7 @@
         }
 
     block_order = ((1, 1), (1, 0), (0, 1), (0, 0))
-    everyone = [
-        (dz, dr, dc) for dz in range(n_wide) for dr, dc in block_order if (dz, dr, dc) != (0, 0, 0)
-    ]
+    everyone = [(0, 0, 1), (0, 1, 0)] + [(dz, 0, 0) for dz in range(n_wide - 1, 0, -1)]
     barrier = pltpu.get_barrier_semaphore()
     for offset in everyone:
         pl.semaphore_signal(barrier, inc=1, device_id=peer(*offset), device_id_type=MESH)
@@ -141,20 +139,11 @@
 
         lax.fori_loop(0, block_groups, begin, 0)
 
-    loads[0].wait()
-    loads[1].wait()
-    tokens = delta.shape[0]
     half = act_factor.shape[1]
-    limit = n_sub * tokens - padding_ref[0] - c * tokens
-    position = lax.broadcasted_iota(jnp.int32, (tokens, half), 0)
-    projected = jnp.dot(delta[...], delta_factor[...], preferred_element_type=jnp.float32)
-    delta_proj = jnp.where(position < limit, projected, 0.0).astype(jnp.bfloat16)
-
-    loads[2].wait()
     pl.semaphore_wait(barrier, len(everyone))
     diag_rows = pl.ds(pl.multiple_of(c * half, half), half)
     diag_copy = pltpu.make_async_remote_copy(
-        src_ref=act_factor.at[diag_rows, :],
+        src_ref=act_factor_hbm.at[diag_rows, :],
         dst_ref=diag,
         send_sem=diag_sem.at[0],
         recv_sem=diag_sem.at[1],
@@ -166,6 +155,15 @@
     def _():
         diag_copy.start()
 
+    loads[0].wait()
+    loads[1].wait()
+    tokens = delta.shape[0]
+    limit = n_sub * tokens - padding_ref[0] - c * tokens
+    position = lax.broadcasted_iota(jnp.int32, (tokens, half), 0)
+    projected = jnp.dot(delta[...], delta_factor[...], preferred_element_type=jnp.float32)
+    delta_proj = jnp.where(position < limit, projected, 0.0).astype(jnp.bfloat16)
+
+    loads[2].wait()
     loads[3].wait()
     inner_mine[...] = lax.dot_general(
         delta_proj, act[...], (((0,), (0,)), ((), ())), preferred_element_type=jnp.float32
@@ -236,11 +234,23 @@
         copy.wait_recv()
     weights[...] = grad_all[...].astype(jnp.float32).T.astype(jnp.bfloat16)
 
-    score_copies = []
-    for k, (dr, dc) in enumerate(block_order):
-        first = block_at(dr, dc) * block_groups
-
-        def step(t, carry, first=first):
+    def score_copy(k, dz):
+        slot = k * n_wide + dz
+        return pltpu.make_async_remote_copy(
+            src_ref=outgoing.at[k, lax.rem(z + dz, n_wide)],
+            dst_ref=incoming.at[slot],
+            send_sem=score_send_sem.at[slot],
+            recv_sem=score_recv_sem.at[slot],
+            device_id=peer(dz, 1 - k // n_sub, 1 - lax.rem(k, n_sub)),
+            device_id_type=MESH,
+        )
+
+    last = len(block_order) - 1
+
+    def score_block(k, carry):
+        first = block_at(1 - k // n_sub, 1 - lax.rem(k, n_sub)) * block_groups
+
+        def score_group(t, inner_carry):
             query_copy(first + t).wait()
             span = pl.ds(pl.multiple_of((first + t) * chunk, chunk), chunk)
             products = jnp.dot(
@@ -251,9 +261,9 @@
                 chosen = jnp.where((tile_of_lane == a)[None], products[:, a], chosen)
             chosen = jnp.where(on_diagonal[None], chosen, 0.0)
             folded[pl.ds(pl.multiple_of(t * GROUP, GROUP), GROUP), :] = jnp.sum(chosen, axis=1)
-            return carry
-
-        lax.fori_loop(0, block_groups, step, 0)
+            return inner_carry
+
+        lax.fori_loop(0, block_groups, score_group, 0)
         sums = folded[...]
         sums_high = sums.astype(jnp.bfloat16)
         sums_low = (sums - sums_high.astype(jnp.float32)).astype(jnp.bfloat16)
@@ -263,29 +273,25 @@
         ) + lax.dot_general(places, sums_low, contract, preferred_element_type=jnp.float32)
         for p in range(n_wide):
             outgoing[k, p] = ranked[p : p + 1, :]
-        for dz in range(n_wide - 1, -1, -1):
-            slot = k * n_wide + dz
-            source = outgoing.at[k, lax.rem(z + dz, n_wide)]
-            if (dz, dr, dc) == (0, 0, 0):
-                continue
-            copy = pltpu.make_async_remote_copy(
-                src_ref=source,
-                dst_ref=incoming.at[slot],
-                send_sem=score_send_sem.at[slot],
-                recv_sem=score_recv_sem.at[slot],
-                device_id=peer(dz, dr, dc),
-                device_id_type=MESH,
-            )
-            copy.start()
-            score_copies.append((slot, copy))
-
-    result = outgoing[len(block_order) - 1, z]
+        for dz in range(n_wide - 1, 0, -1):
+            score_copy(k, dz).start()
+
+        @pl.when(k < last)
+        def _():
+            score_copy(k, 0).start()
+
+        return carry
+
+    lax.fori_loop(0, len(block_order), score_block, 0)
+
+    result = outgoing[last, z]
     for copy in grad_copies:
         copy.wait_send()
-    for slot, copy in score_copies:
-        copy.wait_send()
-        copy.wait_recv()
-        result = result + incoming[slot]
+    for k in range(last + 1):
+        for dz in range(n_wide - 1, -1, -1):
+            if (k, dz) != (last, 0):
+                score_copy(k, dz).wait()
+                result = result + incoming[k * n_wide + dz]
     out_ref[...] = result[:, :block_size]
 
 

time: 39.7 us -> 33.5 us (0.84)
  Pallas kernels: 37.6 us -> 31.4 us
    pallas_call x1, Pallas kernels: 37.6 us -> 31.4 us  [fused_shards(): pl.pallas_call(functools.partial(kernel, n_wide, rows), out_shape=jax.Sha...]
where the time goes in v2:
time: 33.5 us; the launch traced here: 33.3 us
  Pallas kernels  31.4 us (94%)
  local copies, waits for them, and re-layouts  1.24 us (4%)
  between operations  0.66 us (2%)
    pallas_call x1, Pallas kernels, fused_shards(): pl.pallas_call(functools.partial(kernel, n_wide, rows), out_shape=jax.Sha...  31.4 us
    unnamed x1, local copies, waits for them, and re-layouts  1.24 us

profile of v2, /device:TPU:0, one launch (start us, length us, event | category | flops | bytes accessed | tf_op | source)
XLA Modules:
  0.0 33.3 jit_solution(18096392814171494864)
XLA Ops:
  0.7 31.4 %shard_map.73 = f32[1,320]{1,0:T(1,128)} custom-call(s32[4]{0:T(128)} %assignment_ref.1, s32[1]{0:T(128)S(6)} %copy.9.padding_ref, bf16[1024,512]{1,0:T(8,128)(2,1)} %bitcast.4, bf16[1024,512]{1,0:T(8,128)(2,1)} %bitcast.5, bf16[512,256]{1,0:T(8,128)(2,1)} %act_factor_hbm.1, bf16[512,256]{1,0:T(8,128)(2,1)} %delta_factor_hbm.1, bf16[81920,256]{1,0:T(8,128)(2,1)} %bitcast.3), custom_call_target="tpu_custom_call" | custom-call | tf_op jit(solution)/shard_map/pallas_call | solution.py:312
  32.1 1.2 %copy.10 = f32[1,320]{1,0:T(1,128)} copy(f32[1,320]{1,0:T(1,128)} %shard_map.73) | data formatting | bytes 2560

commit v3 on v2

--- a/solution.py
+++ b/solution.py
@@ -130,15 +130,6 @@
     def block_at(dr, dc):
         return lax.rem(r + dr, n_rep) * n_sub + lax.rem(c + dc, n_sub)
 
-    for dr, dc in block_order:
-        first = block_at(dr, dc) * block_groups
-
-        def begin(t, carry, first=first):
-            query_copy(first + t).start()
-            return carry
-
-        lax.fori_loop(0, block_groups, begin, 0)
-
     half = act_factor.shape[1]
     pl.semaphore_wait(barrier, len(everyone))
     diag_rows = pl.ds(pl.multiple_of(c * half, half), half)
@@ -165,6 +156,15 @@
 
     loads[2].wait()
     loads[3].wait()
+    for dr, dc in block_order:
+        first = block_at(dr, dc) * block_groups
+
+        def begin(t, carry, first=first):
+            query_copy(first + t).start()
+            return carry
+
+        lax.fori_loop(0, block_groups, begin, 0)
+
     inner_mine[...] = lax.dot_general(
         delta_proj, act[...], (((0,), (0,)), ((), ())), preferred_element_type=jnp.float32
     )

time: 33.5 us -> 33.5 us (level)
  no operation moved by 1% of the time
where the time goes in v3:
time: 33.5 us; the launch traced here: 33.3 us
  Pallas kernels  31.4 us (94%)
  local copies, waits for them, and re-layouts  1.24 us (4%)
  between operations  0.66 us (2%)
    pallas_call x1, Pallas kernels, fused_shards(): pl.pallas_call(functools.partial(kernel, n_wide, rows), out_shape=jax.Sha...  31.4 us
    unnamed x1, local copies, waits for them, and re-layouts  1.24 us

profile of v3, /device:TPU:0, one launch (start us, length us, event | category | flops | bytes accessed | tf_op | source)
XLA Modules:
  0.0 33.3 jit_solution(17629002265065848258)
XLA Ops:
  0.7 31.4 %shard_map.73 = f32[1,320]{1,0:T(1,128)} custom-call(s32[4]{0:T(128)} %assignment_ref.1, s32[1]{0:T(128)S(6)} %copy.9.padding_ref, bf16[1024,512]{1,0:T(8,128)(2,1)} %bitcast.4, bf16[1024,512]{1,0:T(8,128)(2,1)} %bitcast.5, bf16[512,256]{1,0:T(8,128)(2,1)} %act_factor_hbm.1, bf16[512,256]{1,0:T(8,128)(2,1)} %delta_factor_hbm.1, bf16[81920,256]{1,0:T(8,128)(2,1)} %bitcast.3), custom_call_target="tpu_custom_call" | custom-call | tf_op jit(solution)/shard_map/pallas_call | solution.py:312
  32.1 1.2 %copy.10 = f32[1,320]{1,0:T(1,128)} copy(f32[1,320]{1,0:T(1,128)} %shard_map.73) | data formatting | bytes 2560
